TPU v7x, 512 devices: a whole 4x4x16 slice. The times are simulated.
512 devices in a mesh: dom: 512 (over y, z, x, core).
Axes of the slice: x: 4, y: 4, z: 16, core: 2. Of those that a mesh axis runs over, the one named last changes fastest.
Arguments:
- dof_values: float32 [9, 20, 131072], P(None, None, 'dom'), may hold values from -6 to 6
- star_mats: bfloat16 [3, 9, 9, 131072], P(None, None, None, 'dom'), may hold values from -0.1796875 to 0.1796875
- flux_local: bfloat16 [4, 9, 9, 131072], P(None, None, None, 'dom'), may hold values from -0.19921875 to 0.19921875
- flux_neigh: bfloat16 [4, 9, 9, 131072], P(None, None, None, 'dom'), may hold values from -0.19921875 to 0.19921875
- kstiff: float32 [3, 20, 20], replicated, may hold values from -1.25 to 1.25
- flux_minus: float32 [4, 20, 20], replicated, may hold values from -1.25 to 1.25
- flux_plus: float32 [4, 4, 20, 20], replicated, may hold values from -1.25 to 1.25
- neighbour: int32 [4, 131072], P(None, 'dom'), may hold values from 0 to 511, as said below
- neigh_face: int32 [4, 131072], P(None, 'dom'), may hold values from 0 to 3
- cluster: int32 [131072], P('dom'), may hold values from 0 to 1
- send_list: int32 [512, 4, 64], P('dom'), may hold values from 0 to 255
- damage_list: int32 [512, 256], P('dom'), may hold values from 0 to 255, as said below
- damage_count: int32 [512], P('dom'), may hold values from 0 to 256, as said below
- yield_mask: int32 [20, 131072], P(None, 'dom'), may hold values 0 or 1
- cohesion: float32 [131072], P('dom'), may hold values from 0.3 to 3
- to_points: float32 [20, 20], replicated, may hold values from -1.25 to 1.25
- from_points: float32 [20, 20], replicated, may hold values from -1.25 to 1.25
Outputs:
- new_dofs: float32 [9, 20, 131072], P(None, None, 'dom')
Inputs may be any that keep to these rules, and one draw needn't show every extreme that they name: `neighbour`: entries below 256 are elements of the same partition; the entry 256 + j * 64 + i names ghost slot i of offset slot j. `damage_list`: the entries of one partition's row are distinct. `damage_count`: some partition has exactly 256.
All inputs are finite; a program needn't handle non-finite values. No bound on the sum of `yield_mask` on one device may be relied on, other than what follows from the above.
Results may differ from a plain program's by a relative error of at most 0.0003.
Values sent between devices are 32-bit elements; how exact they have to be, the bound alone decides.
A program may use at most 128 MiB of HBM per device.

v0:
```python
import jax
import jax.numpy as jnp
from jax import lax
from jax.sharding import PartitionSpec as P

NDER = 3
BLK = 128


PRECISE = lax.Precision.HIGHEST
OFFSETS = (1, -1, 2, -2)
FRICTION = 0.6
RELAXATION = 0.5


def from_behind(block, axis, distance):
    devices = range(lax.axis_size(axis))
    route = [(i - distance, i) for i in devices if i - distance in devices]
    return lax.ppermute(block, axis, route)


def star_apply(source, matrix):
    wide = matrix.astype(jnp.float32)
    total = source[0][None, :, :] * wide[0][:, None, :]
    for quantity in range(1, source.shape[0]):
        total = total + source[quantity][None, :, :] * wide[quantity][:, None, :]
    return total


def derivatives(source, star_part, kstiff):
    series = [source]
    for degree in range(NDER - 1):
        latest = series[-1]
        following = jnp.zeros_like(latest)
        for direction in range(3):
            rotated = star_apply(latest, star_part[direction])
            following = following + jnp.einsum(
                "bc,pce->pbe", kstiff[direction], rotated, precision=PRECISE
            )
        series.append(following)
    return series


def taylor(series, time_begin, time_end):
    summed = jnp.zeros_like(series[0])
    divisor = 1.0
    for degree in range(len(series)):
        divisor = divisor * (degree + 1)
        weight_now = (time_end ** (degree + 1) - time_begin ** (degree + 1)) / divisor
        summed = summed + weight_now * series[degree]
    return summed


def volume(integral, star_part, kstiff):
    summed = jnp.zeros_like(integral)
    for direction in range(3):
        rotated = star_apply(integral, star_part[direction])
        summed = summed + jnp.einsum("cb,pce->pbe", kstiff[direction], rotated, precision=PRECISE)
    return summed


def face_values(extended, neighbours):
    return jnp.stack([jnp.take(extended, neighbours[face_id], axis=2) for face_id in range(4)])


def surface(integral, others, neigh_faces, local_flux, neigh_flux, flux_minus, flux_plus):
    summed = jnp.zeros_like(integral)
    for face_id in range(4):
        own_side = star_apply(integral, local_flux[face_id])
        summed = summed + jnp.einsum(
            "bc,pce->pbe", flux_minus[face_id], own_side, precision=PRECISE
        )
        far_side = star_apply(others[face_id], neigh_flux[face_id])
        selector = (
            neigh_faces[face_id][None, :] == jnp.arange(4, dtype=jnp.int32)[:, None]
        ).astype(jnp.float32)
        masked = far_side[None] * selector[:, None, None, :]
        summed = summed + jnp.einsum("hbc,hpce->pbe", flux_plus[face_id], masked, precision=PRECISE)
    return summed


def plastic(stress, strength, plastic_mask, to_points, from_points):
    points = jnp.einsum("nb,qbp->qnp", to_points, stress, precision=PRECISE)
    pressure = (points[0] + points[1] + points[2]) / 3.0
    normal = points[:3] - pressure[None]
    shear_part = points[3:]
    tau_eff = jnp.sqrt(
        0.5 * jnp.sum(normal * normal, axis=0) + jnp.sum(shear_part * shear_part, axis=0)
    )
    yield_limit = jnp.maximum(strength[None, :] - FRICTION * pressure, 0.5 * strength[None, :])
    rate_now = jnp.where(
        plastic_mask > 0.5,
        RELAXATION * (yield_limit / jnp.maximum(tau_eff, yield_limit) - 1.0),
        0.0,
    )
    change = jnp.concatenate([normal, shear_part], axis=0) * rate_now[None]
    return jnp.einsum("bn,qnp->qbp", from_points, change, precision=PRECISE)


def exchange_ghosts(buffer, send_list):
    pieces = []
    for slot_id in range(len(OFFSETS)):
        outgoing = jnp.take(buffer, send_list[0, slot_id], axis=2)
        pieces.append(from_behind(outgoing, "dom", OFFSETS[slot_id]))
    return jnp.concatenate(pieces, axis=2)


def run_blocks(stress, strength, plastic_mask, live_count, to_points, from_points):
    summed = jnp.zeros_like(stress)
    block_count = (live_count + BLK - 1) // BLK

    def one_block(block_id, carried):
        first_row = block_id * BLK
        result_part = plastic(
            lax.dynamic_slice_in_dim(stress, first_row, BLK, 2),
            lax.dynamic_slice_in_dim(strength, first_row, BLK, 0),
            lax.dynamic_slice_in_dim(plastic_mask, first_row, BLK, 1),
            to_points,
            from_points,
        )
        live_slots = (first_row + jnp.arange(BLK, dtype=jnp.int32) < live_count).astype(jnp.float32)
        return lax.dynamic_update_slice_in_dim(
            carried, result_part * live_slots[None, None, :], first_row, 2
        )

    return lax.fori_loop(0, block_count, one_block, summed)


def per_device(
    dof_values,
    star_mats,
    flux_local,
    flux_neigh,
    kstiff,
    flux_minus,
    flux_plus,
    neighbour,
    neigh_face,
    cluster,
    send_list,
    damage_list,
    damage_count,
    yield_mask,
    cohesion,
    to_points,
    from_points,
):
    is_fine = (cluster == 0)[None, None, :]
    first_series = derivatives(dof_values, star_mats, kstiff)
    buffer_one = taylor(first_series, 0.0, 1.0)
    ghost_one = exchange_ghosts(buffer_one, send_list)
    others = face_values(jnp.concatenate([buffer_one, ghost_one], axis=2), neighbour)
    updated = (
        dof_values
        + volume(buffer_one, star_mats, kstiff)
        - surface(buffer_one, others, neigh_face, flux_local, flux_neigh, flux_minus, flux_plus)
    )
    state_one = jnp.where(is_fine, updated, dof_values)
    second_series = derivatives(state_one, star_mats, kstiff)
    buffer_two = jnp.where(
        is_fine, taylor(second_series, 0.0, 1.0), taylor(second_series, 1.0, 2.0)
    )
    ghost_two = exchange_ghosts(buffer_two, send_list)
    summed_buffer = buffer_one + buffer_two
    fine_side = face_values(jnp.concatenate([buffer_two, ghost_two], axis=2), neighbour)
    coarse_side = face_values(
        jnp.concatenate([summed_buffer, ghost_one + ghost_two], axis=2), neighbour
    )
    others = jnp.where(is_fine[None], fine_side, coarse_side)
    integral = jnp.where(is_fine, buffer_two, summed_buffer)
    state_two = (
        state_one
        + volume(integral, star_mats, kstiff)
        - surface(integral, others, neigh_face, flux_local, flux_neigh, flux_minus, flux_plus)
    )
    listing = damage_list[0]
    live_count = damage_count[0]
    stress = jnp.take(state_two[:6], listing, axis=2)
    strength = jnp.take(cohesion, listing)
    plastic_mask = jnp.take(yield_mask, listing, axis=1).astype(jnp.float32)
    correction = run_blocks(stress, strength, plastic_mask, live_count, to_points, from_points)
    return state_two.at[:6, :, listing].add(correction)


def solution(mesh):
    return jax.shard_map(
        per_device,
        mesh=mesh,
        in_specs=(
            P(None, None, "dom"),
            P(None, None, None, "dom"),
            P(None, None, None, "dom"),
            P(None, None, None, "dom"),
            P(),
            P(),
            P(),
            P(None, "dom"),
            P(None, "dom"),
            P("dom"),
            P("dom", None, None),
            P("dom", None),
            P("dom"),
            P(None, "dom"),
            P("dom"),
            P(),
            P(),
        ),
        out_specs=P(None, None, "dom"),
        check_vma=False,
    )
```

profile of v0, /device:TPU:24, one launch (start us, length us, event | category | flops | bytes accessed | tf_op | source)
XLA Modules:
  0.0 1772.6 jit_solution(16652583317750710601)
XLA Ops:
  12.9 13.2 collective-permute-start.1
  31.1 8.1 collective-permute-start.3
  60.5 3.8 copy.185
  64.4 3.1 gather_fusion.7
  69.4 3.0 gather_fusion.8
  79.7 3.1 gather_fusion.9
  90.1 2.9 gather_fusion.10
  121.7 7.9 collective-permute-start.5
  133.0 8.1 collective-permute-start.7
  144.0 4.1 copy.250
  148.2 4.3 gather_fusion.15
  152.4 4.2 gather_fusion.16
  158.0 3.7 copy.258
  161.7 4.3 gather_fusion.19
  165.9 4.3 gather_fusion.20
  170.2 4.3 gather_fusion.17
  174.5 4.3 gather_fusion.21
  178.8 4.3 gather_fusion.18
  183.0 4.3 gather_fusion.22
  187.3 3.6 select_bitcast_fusion.3
  193.5 3.6 select_bitcast_fusion.2
  199.7 3.7 select_bitcast_fusion.1
  206.0 3.7 select_bitcast_fusion
  231.0 1540.3 %while.14 = (s32[]{:T(128)}, f32[9,20,256]{1,2,0:T(8,128)S(1)}, s32[256,2]{0,1:T(2,128)S(1)}, f32[256,6,20]{2,0,1:T(8,128)S(1)}, s32[]{:T(128)}, /*index=5*/s32[3]{0:T(128)S(1)}, s32[1]{0:T(128)}, s32[]{:T(128)}) while((s32[]{:T(128)}, f32[9,20,256]{1,2,0:T(8,128)S(1)}, s32[256,2]{0,1:T(2,128)S(1)}, f32[256,6,20]{2,0,1:T(8,128)S(1)}, s32[]{:T(128)}, ...), condition=%wide.while_cond, body=%wide.while_body.sunk | while | flops 259 | bytes 2563 | solution.py:182
  (2231 shorter events, 1648.5 us)
Async XLA Ops:
  0.0 53.3 %copy-start = (f32[256]{0:T(256)S(1)}, f32[256]{0:T(256)}, u32[]{:S(2)}) copy-start(f32[256]{0:T(256)} %param.37) | copy-start | bytes 3076
  8.9 50.4 %collective-permute-start = (f32[9,20,64]{2,1,0:T(8,128)}, f32[9,20,64]{2,1,0:T(8,128)}, u32[]{:S(2)}, u32[]{:S(2)}) collective-permute-start(f32[9,20,64]{2,1,0:T(8,128)} %select_bitcast_fusion.20), channel_id=1, source_target_pairs={{0,1},{1,2},{2,3},{3,4},{4,5},{5,6},{6,7},{7,8},{8,9},{9,10},{10,1... | collective-permute-start | bytes 138248 | tf_op jit(solution)/shard_map/ppermute | solution.py:19
  12.9 46.4 %collective-permute-start.1 = (f32[9,20,64]{2,1,0:T(8,128)}, f32[9,20,64]{2,1,0:T(8,128)}, u32[]{:S(2)}, u32[]{:S(2)}) collective-permute-start(f32[9,20,64]{2,1,0:T(8,128)} %select_bitcast_fusion.19), channel_id=1, source_target_pairs={{1,0},{2,1},{3,2},{4,3},{5,4},{6,5},{7,6},{8,7},{9,8},{10,9},{11,1... | collective-permute-start | bytes 138248 | tf_op jit(solution)/shard_map/ppermute | solution.py:19
  28.3 31.0 %collective-permute-start.2 = (f32[9,20,64]{2,1,0:T(8,128)}, f32[9,20,64]{2,1,0:T(8,128)}, u32[]{:S(2)}, u32[]{:S(2)}) collective-permute-start(f32[9,20,64]{2,1,0:T(8,128)} %select_bitcast_fusion.18), channel_id=1, source_target_pairs={{0,2},{1,3},{2,4},{3,5},{4,6},{5,7},{6,8},{7,9},{8,10},{9,11},{10,... | collective-permute-start | bytes 138248 | tf_op jit(solution)/shard_map/ppermute | solution.py:19
  31.1 28.1 %collective-permute-start.3 = (f32[9,20,64]{2,1,0:T(8,128)S(1)}, f32[9,20,64]{2,1,0:T(8,128)S(1)}, u32[]{:S(2)}, u32[]{:S(2)}) collective-permute-start(f32[9,20,64]{2,1,0:T(8,128)S(1)} %select_bitcast_fusion.17), channel_id=1, source_target_pairs={{2,0},{3,1},{4,2},{5,3},{6,4},{7,5},{8,6},{9,7},{10,8},{11,9},{12,... | collective-permute-start | bytes 138248 | tf_op jit(solution)/shard_map/ppermute | solution.py:19
  43.4 52.2 %copy-start.9 = (f32[1,4,20,20]{3,1,2,0:T(4,128)}, f32[1,4,20,20]{3,1,2,0:T(4,128)S(1)}, u32[]{:S(2)}) copy-start(f32[1,4,20,20]{3,1,2,0:T(4,128)S(1)} %get-tuple-element.357) | copy-start | bytes 19204
  43.4 53.3 %copy-start.7 = (f32[1,4,20,20]{3,1,2,0:T(4,128)}, f32[1,4,20,20]{3,1,2,0:T(4,128)S(1)}, u32[]{:S(2)}) copy-start(f32[1,4,20,20]{3,1,2,0:T(4,128)S(1)} %get-tuple-element.359) | copy-start | bytes 19204
  43.4 54.4 %copy-start.5 = (f32[1,4,20,20]{3,1,2,0:T(4,128)}, f32[1,4,20,20]{3,1,2,0:T(4,128)S(1)}, u32[]{:S(2)}) copy-start(f32[1,4,20,20]{3,1,2,0:T(4,128)S(1)} %get-tuple-element.358) | copy-start | bytes 19204
  46.4 50.0 %copy-start.109 = (f32[9,256]{1,0:T(8,128)}, f32[9,256]{1,0:T(8,128)S(1)}, u32[]{:S(2)}) copy-start(f32[9,256]{1,0:T(8,128)S(1)} %get-tuple-element.406) | copy-start | bytes 27652
  46.4 50.0 %copy-start.111 = (f32[9,256]{1,0:T(8,128)}, f32[9,256]{1,0:T(8,128)S(1)}, u32[]{:S(2)}) copy-start(f32[9,256]{1,0:T(8,128)S(1)} %get-tuple-element.407) | copy-start | bytes 27652
  46.4 50.0 %copy-start.113 = (f32[9,256]{1,0:T(8,128)}, f32[9,256]{1,0:T(8,128)S(1)}, u32[]{:S(2)}) copy-start(f32[9,256]{1,0:T(8,128)S(1)} %get-tuple-element.408) | copy-start | bytes 27652
  46.4 50.0 %copy-start.115 = (f32[9,256]{1,0:T(8,128)}, f32[9,256]{1,0:T(8,128)S(1)}, u32[]{:S(2)}) copy-start(f32[9,256]{1,0:T(8,128)S(1)} %get-tuple-element.409) | copy-start | bytes 27652
  46.4 50.0 %copy-start.117 = (f32[9,256]{1,0:T(8,128)}, f32[9,256]{1,0:T(8,128)S(1)}, u32[]{:S(2)}) copy-start(f32[9,256]{1,0:T(8,128)S(1)} %get-tuple-element.410) | copy-start | bytes 27652
  46.4 50.0 %copy-start.119 = (f32[9,256]{1,0:T(8,128)}, f32[9,256]{1,0:T(8,128)S(1)}, u32[]{:S(2)}) copy-start(f32[9,256]{1,0:T(8,128)S(1)} %get-tuple-element.411) | copy-start | bytes 27652
  46.4 50.0 %copy-start.121 = (f32[9,256]{1,0:T(8,128)}, f32[9,256]{1,0:T(8,128)S(1)}, u32[]{:S(2)}) copy-start(f32[9,256]{1,0:T(8,128)S(1)} %get-tuple-element.412) | copy-start | bytes 27652
  46.4 50.0 %copy-start.123 = (f32[9,256]{1,0:T(8,128)}, f32[9,256]{1,0:T(8,128)S(1)}, u32[]{:S(2)}) copy-start(f32[9,256]{1,0:T(8,128)S(1)} %get-tuple-element.413) | copy-start | bytes 27652
  46.5 50.1 %copy-start.203 = (f32[4,256]{1,0:T(4,128)}, f32[4,256]{1,0:T(4,128)S(1)}, u32[]{:S(2)}) copy-start(f32[4,256]{1,0:T(4,128)S(1)} %fusion.1012) | copy-start | bytes 12292
  47.9 49.9 %copy-start.202 = (f32[4,256]{1,0:T(4,128)}, f32[4,256]{1,0:T(4,128)S(1)}, u32[]{:S(2)}) copy-start(f32[4,256]{1,0:T(4,128)S(1)} %fusion.1013) | copy-start | bytes 12292
  52.6 51.6 %copy-start.19 = (f32[9,256]{1,0:T(8,128)}, f32[9,256]{1,0:T(8,128)S(1)}, u32[]{:S(2)}) copy-start(f32[9,256]{1,0:T(8,128)S(1)} %get-tuple-element.361) | copy-start | bytes 27652
  117.8 26.0 %collective-permute-start.4 = (f32[9,20,64]{2,1,0:T(8,128)S(1)}, f32[9,20,64]{2,1,0:T(8,128)S(1)}, u32[]{:S(2)}, u32[]{:S(2)}) collective-permute-start(f32[9,20,64]{2,1,0:T(8,128)S(1)} %select_bitcast_fusion.16), channel_id=1, source_target_pairs={{0,1},{1,2},{2,3},{3,4},{4,5},{5,6},{6,7},{7,8},{8,9},{9,10},{10,1... | collective-permute-start | bytes 138248 | tf_op jit(solution)/shard_map/ppermute | solution.py:19
  121.7 22.1 %collective-permute-start.5 = (f32[9,20,64]{2,1,0:T(8,128)S(1)}, f32[9,20,64]{2,1,0:T(8,128)S(1)}, u32[]{:S(2)}, u32[]{:S(2)}) collective-permute-start(f32[9,20,64]{2,1,0:T(8,128)S(1)} %select_bitcast_fusion.15), channel_id=1, source_target_pairs={{1,0},{2,1},{3,2},{4,3},{5,4},{6,5},{7,6},{8,7},{9,8},{10,9},{11,1... | collective-permute-start | bytes 138248 | tf_op jit(solution)/shard_map/ppermute | solution.py:19
  130.8 13.0 collective-permute-start.6
  133.0 10.8 collective-permute-start.7
  230.7 1541.7 %copy-start.1 = (f32[256]{0:T(256)S(1)}, f32[256]{0:T(256)}, u32[]{:S(2)}) copy-start(f32[256]{0:T(256)} %param.37) | copy-start | bytes 3076
  (333 other events, 2668.1 us)
where the time goes:
time: 1800 us; the launch traced here: 1770 us
  other arithmetic  1050 us (58%)
  local copies, waits for them, and re-layouts  633 us (35%)
  starting transfers between devices  45 us (2%)
  matrix products  26.7 us (1%)
    scatter-add x512, other arithmetic  1020 us
    scatter-add x768, local copies, waits for them, and re-layouts  511 us
    gather x12, local copies, waits for them, and re-layouts, face_values(): jnp.take(extended, neighbours[face_id], axis=2)  46.2 us
    ppermute x8, starting transfers between devices, from_behind(): return lax.ppermute(block, axis, route)  45 us
  transfers between devices with their start and end apart: 8, of which 0 were waited for; matrix products, arithmetic and copies ran while one was open for 2% of the time, Pallas kernels for 0%

commit v1 on v0

v1 whole, which is shorter than its diff:
```python
import functools

import jax
import jax.numpy as jnp
from jax import lax
from jax.experimental import pallas as pl
from jax.experimental.pallas import tpu as pltpu
from jax.sharding import PartitionSpec as P

F32, BF16 = jnp.float32, jnp.bfloat16
MESH = pl.DeviceIdType.MESH
OFFSETS = (1, -1, 2, -2)
NQ, NBAS, PAD = 9, 20, 24
ROWS = NQ * PAD
GROUP = 3 * PAD
E, NB = 256, 64
TOP = 112
FRICTION, RELAXATION = 0.6, 0.5


def iota(shape, dim):
    return lax.broadcasted_iota(jnp.int32, shape, dim)


def halves(x):
    hi = x.astype(BF16).astype(F32)
    return hi, x - hi


def right_side(hi, lo):
    rest = jnp.zeros((256 - 3 * GROUP, E), F32)
    return jnp.concatenate([hi, lo, hi, rest], axis=0).astype(BF16)


def dot(a, b):
    return jnp.dot(a, b, preferred_element_type=F32)


def pad_rows(m):
    return jnp.concatenate([m, jnp.zeros((PAD - NBAS, m.shape[1]), F32)], axis=0)


def left_side(mats):
    stacked = jnp.concatenate([pad_rows(m) for m in mats], axis=0)
    hi, lo = halves(stacked)
    lane, row = iota((NBAS, 256), 1), iota((NBAS, 256), 0)
    here = lax.rem(lane, PAD) == row
    one, zero = jnp.ones((NBAS, 256), F32), jnp.zeros((NBAS, 256), F32)
    to_hi = jnp.where(here & (lane < 2 * GROUP), one, zero).astype(BF16)
    to_lo = jnp.where(here & (lane >= 2 * GROUP) & (lane < 3 * GROUP), one, zero).astype(BF16)
    spread = dot(hi.astype(BF16), to_hi) + dot(lo.astype(BF16), to_lo)
    owner = lax.rem(lax.div(iota(spread.shape, 1), PAD), 3)
    blocks = [jnp.where(owner == q, spread, jnp.zeros_like(spread)) for q in range(3)]
    return jnp.concatenate(blocks, axis=0).astype(BF16)


def transposed(m):
    hi, lo = halves(m)
    eye = (iota((NBAS, NBAS), 0) == iota((NBAS, NBAS), 1)).astype(F32).astype(BF16)
    dims = (((1,), (1,)), ((), ()))
    return lax.dot_general(eye, hi.astype(BF16), dims, preferred_element_type=F32) + lax.dot_general(
        eye, lo.astype(BF16), dims, preferred_element_type=F32
    )


def kernel(
    n, dof, star, flux_l, flux_n, kst, f_minus, f_plus, neigh, nface, clus, send_l, dmg, count, ymask, coh, to_p, from_p,
    out, bd_d, bd_o, bd_f, bd_p, coef, onehot, onehot_s, x, x1, st, buf, c1, y, z, ext, ghost, send, recv, ssem, rsem,
):
    me = lax.axis_index("dom")
    barrier = pltpu.get_barrier_semaphore()
    for o in OFFSETS:
        pl.semaphore_signal(barrier, inc=1, device_id=(lax.rem(me + o + n, n),), device_id_type=MESH)

    for q in range(NQ):
        x[PAD * q : PAD * (q + 1), :] = pad_rows(dof[q])

    def widen(q, _):
        for d in range(3):
            coef[d, q] = star[d, q].astype(F32)
        return 0

    lax.fori_loop(0, NQ, widen, 0)
    bd_d[...] = left_side([kst[d] for d in range(3)])
    for j in range(4):
        listed = send_l[0, j : j + 1, :]
        if j % 2 == 0:
            first = listed
        else:
            both = jnp.concatenate([first, listed], axis=1)
            lanes = slice(128 * (j // 2), 128 * (j // 2) + 128)
            onehot_s[:, lanes] = (iota((E, 128), 0) == both).astype(F32).astype(BF16)

    def spread(src, lhs, dst):
        rows = lhs.shape[0]
        for g in range(3):
            dst[rows * g : rows * (g + 1), :] = dot(
                lhs[...], right_side(*halves(src[GROUP * g : GROUP * (g + 1), :]))
            )

    def accumulate(y_ref, row_of, nk, kbase, lanes, accs):
        def step(q, accs):
            accs = list(accs)
            for k in range(nk):
                yv = y_ref[pl.ds(pl.multiple_of(row_of(q, k), 8), PAD), lanes]
                for p in range(NQ):
                    accs[p] = accs[p] + yv * coef[kbase + k, q, p : p + 1, lanes]
            return tuple(accs)

        return lax.fori_loop(0, NQ, step, tuple(accs))

    def zeros9():
        return [jnp.zeros((PAD, 128), F32)] * NQ

    def predictor(src, w1, w2):
        spread(src, bd_d, y)
        for t in range(2):
            lanes = slice(128 * t, 128 * t + 128)
            accs = accumulate(y, lambda q, k: (q * 3 + k) * PAD, 3, 0, lanes, zeros9())
            for p in range(NQ):
                x1[PAD * p : PAD * (p + 1), lanes] = accs[p]
        spread(x1, bd_d, y)
        for t in range(2):
            lanes = slice(128 * t, 128 * t + 128)
            accs = accumulate(y, lambda q, k: (q * 3 + k) * PAD, 3, 0, lanes, zeros9())
            for p in range(NQ):
                rows = slice(PAD * p, PAD * (p + 1))
                buf[rows, lanes] = src[rows, lanes] + w1(lanes) * x1[rows, lanes] + w2(lanes) * accs[p]

    def split_field(field):
        pieces = []
        for g in range(3):
            pieces += list(halves(field[GROUP * g : GROUP * (g + 1), :]))
        return jnp.concatenate(pieces, axis=0).astype(BF16)

    def copies(turn):
        return [
            pltpu.make_async_remote_copy(
                src_ref=send.at[turn, j],
                dst_ref=recv.at[turn, j],
                send_sem=ssem.at[turn, j],
                recv_sem=rsem.at[turn, j],
                device_id=(lax.rem(me + o + n, n),),
                device_id_type=MESH,
            )
            for j, o in enumerate(OFFSETS)
        ]

    low = iota((TOP, 128), 1) < NB

    def start_exchange(turn):
        ext[:, 0:E] = split_field(buf)
        picked = dot(ext[:, 0:E], onehot_s[...])
        packed = jnp.concatenate(
            [picked[2 * GROUP * g : 2 * GROUP * g + GROUP] + picked[2 * GROUP * g + GROUP : 2 * GROUP * (g + 1)] for g in range(3)],
            axis=0,
        )
        for t in range(2):
            upper = packed[0:TOP, 128 * t : 128 * t + 128]
            lower = packed[ROWS - TOP : ROWS, 128 * t : 128 * t + 128]
            send[turn, 2 * t] = jnp.where(low, upper, pltpu.roll(lower, NB, 1))
            send[turn, 2 * t + 1] = jnp.where(low, pltpu.roll(upper, NB, 1), lower)
        for copy in copies(turn):
            copy.start()

    def end_exchange(turn):
        for copy in copies(turn):
            copy.wait_recv()
        for t in range(2):
            one, two = recv[turn, 2 * t], recv[turn, 2 * t + 1]
            lanes = slice(128 * t, 128 * t + 128)
            ghost[0:TOP, lanes] = jnp.where(low, one, pltpu.roll(two, NB, 1))
            ghost[ROWS - TOP : ROWS, lanes] = jnp.where(low, pltpu.roll(one, NB, 1), two)
        ext[:, E : 2 * E] = split_field(ghost)

    def own_side():
        spread(buf, bd_o, y)

    def far_side():
        for f in range(4):
            here = [nface[f : f + 1, :] == h for h in range(3)]
            picked = dot(ext[...], onehot[f])
            for g in range(3):
                hi = picked[2 * GROUP * g : 2 * GROUP * g + GROUP]
                lo = picked[2 * GROUP * g + GROUP : 2 * GROUP * (g + 1)]
                four = dot(bd_f[f], right_side(hi, lo))
                for i in range(3):
                    part = [four[PAD * (4 * i + h) : PAD * (4 * i + h + 1)] for h in range(4)]
                    chosen = jnp.where(here[0], part[0], jnp.where(here[1], part[1], jnp.where(here[2], part[2], part[3])))
                    row = f * ROWS + (3 * g + i) * PAD
                    z[row : row + PAD, :] = chosen

    def own_sum(lanes):
        return accumulate(y, lambda q, k: (q * 7 + k) * PAD, 7, 0, lanes, zeros9())

    def far_sum(lanes, accs):
        return accumulate(z, lambda q, k: k * ROWS + q * PAD, 4, 7, lanes, accs)

    predictor(x, lambda lanes: 0.5, lambda lanes: 1.0 / 6.0)
    pl.semaphore_wait(barrier, len(OFFSETS))
    start_exchange(0)

    def widen_flux(q, _):
        for f in range(4):
            coef[3 + f, q] = flux_l[f, q].astype(F32)
            coef[7 + f, q] = flux_n[f, q].astype(F32)
        return 0

    lax.fori_loop(0, NQ, widen_flux, 0)
    bd_o[...] = left_side([transposed(kst[d]) for d in range(3)] + [-f_minus[f] for f in range(4)])
    for f in range(4):
        bd_f[f] = left_side([-f_plus[f, h] for h in range(4)])
    bd_p[0] = left_side([to_p[...]])
    bd_p[1] = left_side([from_p[...]])
    for f in range(4):
        wanted = neigh[f : f + 1, :]
        onehot[f, 0:E, :] = (iota((E, E), 0) == wanted).astype(F32).astype(BF16)
        for j, o in enumerate(OFFSETS):
            source = me - o
            inside = (source >= 0) & (source < n)
            base = jnp.where(inside, E + NB * j, -4 * E)
            rows = slice(E + NB * j, E + NB * (j + 1))
            onehot[f, rows, :] = ((iota((NB, E), 0) + base) == wanted).astype(F32).astype(BF16)

    own_side()
    for t in range(2):
        lanes = slice(128 * t, 128 * t + 128)
        accs = own_sum(lanes)
        for p in range(NQ):
            c1[PAD * p : PAD * (p + 1), lanes] = accs[p]
    end_exchange(0)
    far_side()
    for t in range(2):
        lanes = slice(128 * t, 128 * t + 128)
        accs = far_sum(lanes, [c1[PAD * p : PAD * (p + 1), lanes] for p in range(NQ)])
        fine = clus[0:1, lanes] == 0
        for p in range(NQ):
            rows = slice(PAD * p, PAD * (p + 1))
            start = x[rows, lanes]
            total = start + accs[p]
            c1[rows, lanes] = total
            st[rows, lanes] = jnp.where(fine, total, start)

    def weight(fine_one, coarse_one):
        return lambda lanes: jnp.where(clus[0:1, lanes] == 0, F32(fine_one), F32(coarse_one))

    predictor(st, weight(0.5, 1.5), weight(1.0 / 6.0, 7.0 / 6.0))
    start_exchange(1)
    own_side()
    for t in range(2):
        lanes = slice(128 * t, 128 * t + 128)
        accs = own_sum(lanes)
        for p in range(NQ):
            rows = slice(PAD * p, PAD * (p + 1))
            c1[rows, lanes] = c1[rows, lanes] + accs[p]
    listed = (iota((E, E), 0) == dmg[...]) & (iota((E, E), 1) < count[0])
    live = lax.dot_general(
        jnp.ones((8, E), BF16), listed.astype(F32).astype(BF16), (((1,), (1,)), ((), ())), preferred_element_type=F32
    )[0:1]
    end_exchange(1)
    far_side()
    for t in range(2):
        lanes = slice(128 * t, 128 * t + 128)
        accs = far_sum(lanes, [c1[PAD * p : PAD * (p + 1), lanes] for p in range(NQ)])
        for p in range(NQ):
            c1[PAD * p : PAD * (p + 1), lanes] = accs[p]

    points = []
    for g in range(2):
        got = dot(bd_p[0], right_side(*halves(c1[GROUP * g : GROUP * (g + 1), :])))
        points += [got[PAD * i : PAD * (i + 1)] for i in range(3)]
    pressure = (points[0] + points[1] + points[2]) / 3.0
    dev = [points[i] - pressure for i in range(3)] + points[3:]
    tau = jnp.sqrt(
        0.5 * (dev[0] * dev[0] + dev[1] * dev[1] + dev[2] * dev[2])
        + (dev[3] * dev[3] + dev[4] * dev[4] + dev[5] * dev[5])
    )
    strength = coh[0:1, :]
    limit = jnp.maximum(strength - FRICTION * pressure, 0.5 * strength)
    rate = RELAXATION * (limit / jnp.maximum(tau, limit) - 1.0)
    marked = jnp.concatenate([ymask[...], jnp.zeros((PAD - NBAS, E), jnp.int32)], axis=0)
    rate = jnp.where((marked == 1) & (live > 0.5), rate, jnp.zeros_like(rate))
    for g in range(2):
        change = jnp.concatenate([rate * dev[3 * g + i] for i in range(3)], axis=0)
        got = dot(bd_p[1], right_side(*halves(change)))
        for i in range(3):
            q = 3 * g + i
            out[q] = c1[PAD * q : PAD * q + NBAS, :] + got[PAD * i : PAD * i + NBAS]
    for q in range(6, NQ):
        out[q] = c1[PAD * q : PAD * q + NBAS, :]
    for turn in range(2):
        for copy in copies(turn):
            copy.wait_send()


def per_device(n, dof, star, flux_l, flux_n, kst, fm, fp, neigh, nface, clus, send_l, dmg, count, ymask, coh, to_p, from_p):
    vmem = pl.BlockSpec(memory_space=pltpu.VMEM)
    smem = pl.BlockSpec(memory_space=pltpu.SMEM)
    return pl.pallas_call(
        functools.partial(kernel, n),
        out_shape=jax.ShapeDtypeStruct((NQ, NBAS, E), F32),
        in_specs=[vmem] * 12 + [smem] + [vmem] * 4,
        out_specs=vmem,
        scratch_shapes=[
            pltpu.VMEM((3 * GROUP, 256), BF16),
            pltpu.VMEM((7 * GROUP, 256), BF16),
            pltpu.VMEM((4, 4 * GROUP, 256), BF16),
            pltpu.VMEM((2, GROUP, 256), BF16),
            pltpu.VMEM((11, NQ, NQ, E), F32),
            pltpu.VMEM((4, 2 * E, E), BF16),
            pltpu.VMEM((E, E), BF16),
            pltpu.VMEM((ROWS, E), F32),
            pltpu.VMEM((ROWS, E), F32),
            pltpu.VMEM((ROWS, E), F32),
            pltpu.VMEM((ROWS, E), F32),
            pltpu.VMEM((ROWS, E), F32),
            pltpu.VMEM((7 * ROWS, E), F32),
            pltpu.VMEM((4 * ROWS, E), F32),
            pltpu.VMEM((2 * ROWS, 2 * E), BF16),
            pltpu.VMEM((ROWS, E), F32),
            pltpu.VMEM((2, 4, TOP, 128), F32),
            pltpu.VMEM((2, 4, TOP, 128), F32),
            pltpu.SemaphoreType.DMA((2, 4)),
            pltpu.SemaphoreType.DMA((2, 4)),
        ],
        compiler_params=pltpu.CompilerParams(
            collective_id=0, has_side_effects=True, vmem_limit_bytes=40 << 20
        ),
        name="ader_cycle",
    )(dof, star, flux_l, flux_n, kst, fm, fp, neigh, nface, clus.reshape(1, E), send_l, dmg, count, ymask, coh.reshape(1, E), to_p, from_p)


def solution(mesh):
    n = mesh.shape["dom"]
    return jax.shard_map(
        functools.partial(per_device, n),
        mesh=mesh,
        in_specs=(
            P(None, None, "dom"),
            P(None, None, None, "dom"),
            P(None, None, None, "dom"),
            P(None, None, None, "dom"),
            P(),
            P(),
            P(),
            P(None, "dom"),
            P(None, "dom"),
            P("dom"),
            P("dom", None, None),
            P("dom", None),
            P("dom"),
            P(None, "dom"),
            P("dom"),
            P(),
            P(),
        ),
        out_specs=P(None, None, "dom"),
        check_vma=False,
    )
```

time: 1800 us -> 40.6 us (0.02)
  the two profiles are of different devices: /device:TPU:24 before, /device:TPU:1 now
where the time goes in v1:
time: 40.6 us; the launch traced here: 40.4 us
  Pallas kernels  34.4 us (85%)
  local copies, waits for them, and re-layouts  5.17 us (13%)
  between operations  0.8 us (2%)
    pallas_call x1, Pallas kernels, per_device(): pl.pallas_call(functools.partial(kernel, n), out_shape=jax.ShapeDtypeStru...  34.4 us
    unnamed x34, local copies, waits for them, and re-layouts  5.17 us

profile of v1, /device:TPU:1, one launch (start us, length us, event | category | flops | bytes accessed | tf_op | source)
XLA Modules:
  0.0 40.4 jit_solution(18105483291773820368)
XLA Ops:
  0.7 0.8 %copy.21.f_minus = f32[4,20,20]{2,1,0:T(8,128)S(1)} copy(f32[4,20,20]{2,0,1:T(4,128)} %param.22) | data formatting | bytes 12800 | tf_op args[5]
  1.4 1.0 %copy.22.f_plus = f32[4,4,20,20]{3,2,1,0:T(8,128)S(1)} copy(f32[4,4,20,20]{3,1,2,0:T(4,128)} %param.23) | data formatting | bytes 51200 | tf_op args[6]
  2.4 0.0 copy-done.13
  2.5 0.9 %copy-done.11 = bf16[4,9,9,256]{3,0,2,1:T(4,128)(2,1)S(1)} copy-done((bf16[4,9,9,256]{3,0,2,1:T(4,128)(2,1)S(1)}, bf16[4,9,9,256]{3,0,2,1:T(4,128)(2,1)}, u32[]{:S(2)}) %copy-start.11) | copy-done | bytes 165912
  3.4 0.9 %copy-done.12 = bf16[4,9,9,256]{3,0,2,1:T(4,128)(2,1)S(1)} copy-done((bf16[4,9,9,256]{3,0,2,1:T(4,128)(2,1)S(1)}, bf16[4,9,9,256]{3,0,2,1:T(4,128)(2,1)}, u32[]{:S(2)}) %copy-start.12) | copy-done | bytes 165912
  4.3 0.0 copy-start.4
  4.3 0.0 copy-start.5
  4.3 0.0 copy-start.6
  4.3 0.0 copy-start.7
  4.3 0.0 copy-start.8
  4.3 0.0 copy-start.9
  4.3 0.0 copy-start.10
  4.4 0.8 %copy-done = f32[9,20,256]{2,1,0:T(8,128)S(1)} copy-done((f32[9,20,256]{2,1,0:T(8,128)S(1)}, f32[9,20,256]{2,1,0:T(8,128)}, u32[]{:S(2)}) %copy-start) | copy-done | bytes 184344
  5.2 0.0 copy-done.1
  5.2 0.0 copy-done.2
  5.2 0.0 copy-done.3
  5.2 0.0 copy-done.4
  5.2 0.0 copy-done.5
  5.2 0.0 copy-done.6
  5.2 0.0 copy-done.7
  5.2 0.0 copy-done.8
  5.3 0.0 copy-done.9
  5.3 34.4 %ader_cycle.1 = f32[9,20,256]{2,1,0:T(8,128)S(1)} custom-call(f32[9,20,256]{2,1,0:T(8,128)S(1)} %copy-done, bf16[3,9,9,256]{3,2,1,0:T(8,128)(2,1)S(1)} %copy.18.star, bf16[4,9,9,256]{3,2,1,0:T(8,128)(2,1)S(1)} %copy.19.flux_l, bf16[4,9,9,256]{3,2,1,0:T(8,128)(2,1)S(1)} %copy.20.flux_n, f32[3,20,20]{2,1,0:T(8,128)S(1)} %copy-done.1, ...), custom_call_target="tpu_custom_call" | custom-call | tf_op jit(solution)/shard_map/ader_cycle/pallas_call | solution.py:299
  39.7 0.7 %copy.25 = f32[9,20,256]{2,1,0:T(8,128)} copy(f32[9,20,256]{2,1,0:T(8,128)S(1)} %ader_cycle.1) | data formatting | bytes 368640
  (11 shorter events, 0.1 us)
Async XLA Ops:
  1.4 1.0 %copy-start.13 = (bf16[3,9,9,256]{3,0,2,1:T(4,128)(2,1)S(1)}, bf16[3,9,9,256]{3,0,2,1:T(4,128)(2,1)}, u32[]{:S(2)}) copy-start(bf16[3,9,9,256]{3,0,2,1:T(4,128)(2,1)} %param.18) | copy-start | bytes 373252
  2.4 0.9 %copy-start.11 = (bf16[4,9,9,256]{3,0,2,1:T(4,128)(2,1)S(1)}, bf16[4,9,9,256]{3,0,2,1:T(4,128)(2,1)}, u32[]{:S(2)}) copy-start(bf16[4,9,9,256]{3,0,2,1:T(4,128)(2,1)} %param.19) | copy-start | bytes 497668
  3.3 0.9 %copy-start.12 = (bf16[4,9,9,256]{3,0,2,1:T(4,128)(2,1)S(1)}, bf16[4,9,9,256]{3,0,2,1:T(4,128)(2,1)}, u32[]{:S(2)}) copy-start(bf16[4,9,9,256]{3,0,2,1:T(4,128)(2,1)} %param.20) | copy-start | bytes 497668
  4.3 0.9 %copy-start = (f32[9,20,256]{2,1,0:T(8,128)S(1)}, f32[9,20,256]{2,1,0:T(8,128)}, u32[]{:S(2)}) copy-start(f32[9,20,256]{2,1,0:T(8,128)} %dof.1) | copy-start | bytes 552964
  4.3 0.9 %copy-start.1 = (f32[3,20,20]{2,1,0:T(8,128)S(1)}, f32[3,20,20]{2,1,0:T(8,128)}, u32[]{:S(2)}) copy-start(f32[3,20,20]{2,1,0:T(8,128)} %kst.1) | copy-start | bytes 14404
  4.3 0.9 %copy-start.2 = (s32[20,256]{1,0:T(8,128)S(1)}, s32[20,256]{1,0:T(8,128)}, u32[]{:S(2)}) copy-start(s32[20,256]{1,0:T(8,128)} %ymask.1) | copy-start | bytes 61444
  4.3 0.9 %copy-start.3 = (f32[20,20]{1,0:T(8,128)S(1)}, f32[20,20]{1,0:T(8,128)}, u32[]{:S(2)}) copy-start(f32[20,20]{1,0:T(8,128)} %to_p.1) | copy-start | bytes 4804
  4.3 0.9 %copy-start.4 = (f32[20,20]{1,0:T(8,128)S(1)}, f32[20,20]{1,0:T(8,128)}, u32[]{:S(2)}) copy-start(f32[20,20]{1,0:T(8,128)} %from_p.1) | copy-start | bytes 4804
  4.3 0.9 %copy-start.5 = (s32[4,256]{1,0:T(4,128)S(1)}, s32[4,256]{1,0:T(4,128)}, u32[]{:S(2)}) copy-start(s32[4,256]{1,0:T(4,128)} %neigh.1) | copy-start | bytes 12292
  4.3 0.9 %copy-start.6 = (s32[4,256]{1,0:T(4,128)S(1)}, s32[4,256]{1,0:T(4,128)}, u32[]{:S(2)}) copy-start(s32[4,256]{1,0:T(4,128)} %nface.1) | copy-start | bytes 12292
  4.3 0.9 %copy-start.7 = (s32[1,4,64]{2,1,0:T(4,128)S(1)}, s32[1,4,64]{2,1,0:T(4,128)}, u32[]{:S(2)}) copy-start(s32[1,4,64]{2,1,0:T(4,128)} %send_l.1) | copy-start | bytes 3076
  4.3 0.9 %copy-start.8 = (s32[256]{0:T(256)S(1)}, s32[256]{0:T(256)}, u32[]{:S(2)}) copy-start(s32[256]{0:T(256)} %param.26) | copy-start | bytes 3076
  4.3 0.9 %copy-start.9 = (s32[1,256]{1,0:T(1,128)S(1)}, s32[1,256]{1,0:T(1,128)}, u32[]{:S(2)}) copy-start(s32[1,256]{1,0:T(1,128)} %dmg.1) | copy-start | bytes 3076
  4.3 0.9 %copy-start.10 = (f32[256]{0:T(256)S(1)}, f32[256]{0:T(256)}, u32[]{:S(2)}) copy-start(f32[256]{0:T(256)} %param.31) | copy-start | bytes 3076

commit v2 on v1

--- a/solution.py
+++ b/solution.py
@@ -64,24 +64,56 @@
 
 
 def kernel(
-    n, dof, star, flux_l, flux_n, kst, f_minus, f_plus, neigh, nface, clus, send_l, dmg, count, ymask, coh, to_p, from_p,
-    out, bd_d, bd_o, bd_f, bd_p, coef, onehot, onehot_s, x, x1, st, buf, c1, y, z, ext, ghost, send, recv, ssem, rsem,
+    n, h_dof, h_star, h_flux_l, h_flux_n, h_kst, h_minus, h_plus, h_neigh, h_nface, h_clus, h_send, h_dmg, h_count, h_ymask, h_coh,
+    h_to, h_from, out,
+    dof, star, flux_l, flux_n, kst, f_minus, f_plus, neigh, nface, clus, send_l, dmg, ymask, coh, to_p, from_p, isem,
+    bd_d, bd_o, bd_f, bd_p, coef_s, coef_l, coef_n, onehot, onehot_s, x, x1, st, buf, c1, y, z, ext, ghost, send, recv, ssem, rsem,
 ):
     me = lax.axis_index("dom")
+    pairs = (
+        (h_dof, dof), (h_kst, kst), (h_star, star), (h_send, send_l), (h_plus, f_plus), (h_minus, f_minus), (h_flux_l, flux_l),
+        (h_flux_n, flux_n), (h_neigh, neigh), (h_nface, nface), (h_clus, clus), (h_to, to_p), (h_from, from_p),
+        (h_dmg, dmg), (h_ymask, ymask), (h_coh, coh),
+    )
+    loads = [pltpu.make_async_copy(src, ref, isem.at[i]) for i, (src, ref) in enumerate(pairs)]
+    for load in loads:
+        load.start()
+
+    def arrived(*refs):
+        for ref in refs:
+            for (_, held), load in zip(pairs, loads):
+                if held is ref:
+                    load.wait()
+
+    def inside(device):
+        return (device >= 0) & (device < n)
+
     barrier = pltpu.get_barrier_semaphore()
     for o in OFFSETS:
-        pl.semaphore_signal(barrier, inc=1, device_id=(lax.rem(me + o + n, n),), device_id_type=MESH)
-
+
+        @pl.when(inside(me + o))
+        def _():
+            pl.semaphore_signal(barrier, inc=1, device_id=(me + o,), device_id_type=MESH)
+
+    partners = sum(jnp.where(inside(me + o), 1, 0) for o in OFFSETS)
+    for j, o in enumerate(OFFSETS):
+
+        @pl.when(jnp.logical_not(inside(me - o)))
+        def _():
+            for turn in range(2):
+                recv[turn, j] = jnp.zeros((TOP, 128), F32)
+
+    arrived(dof, kst, star)
     for q in range(NQ):
         x[PAD * q : PAD * (q + 1), :] = pad_rows(dof[q])
 
     def widen(q, _):
-        for d in range(3):
-            coef[d, q] = star[d, q].astype(F32)
+        coef_s[q] = star[q].astype(F32)
         return 0
 
     lax.fori_loop(0, NQ, widen, 0)
     bd_d[...] = left_side([kst[d] for d in range(3)])
+    arrived(send_l)
     for j in range(4):
         listed = send_l[0, j : j + 1, :]
         if j % 2 == 0:
@@ -98,16 +130,20 @@
                 lhs[...], right_side(*halves(src[GROUP * g : GROUP * (g + 1), :]))
             )
 
-    def accumulate(y_ref, row_of, nk, kbase, lanes, accs):
+    def accumulate(y_ref, row_of, coefs, lanes, accs):
         def step(q, accs):
             accs = list(accs)
-            for k in range(nk):
+            for k, (coef, i) in enumerate(coefs):
                 yv = y_ref[pl.ds(pl.multiple_of(row_of(q, k), 8), PAD), lanes]
                 for p in range(NQ):
-                    accs[p] = accs[p] + yv * coef[kbase + k, q, p : p + 1, lanes]
+                    accs[p] = accs[p] + yv * coef[q, p, i : i + 1, lanes]
             return tuple(accs)
 
         return lax.fori_loop(0, NQ, step, tuple(accs))
+
+    star_coefs = [(coef_s, d) for d in range(3)]
+    own_coefs = star_coefs + [(coef_l, f) for f in range(4)]
+    far_coefs = [(coef_n, f) for f in range(4)]
 
     def zeros9():
         return [jnp.zeros((PAD, 128), F32)] * NQ
@@ -116,13 +152,13 @@
         spread(src, bd_d, y)
         for t in range(2):
             lanes = slice(128 * t, 128 * t + 128)
-            accs = accumulate(y, lambda q, k: (q * 3 + k) * PAD, 3, 0, lanes, zeros9())
+            accs = accumulate(y, lambda q, k: (q * 3 + k) * PAD, star_coefs, lanes, zeros9())
             for p in range(NQ):
                 x1[PAD * p : PAD * (p + 1), lanes] = accs[p]
         spread(x1, bd_d, y)
         for t in range(2):
             lanes = slice(128 * t, 128 * t + 128)
-            accs = accumulate(y, lambda q, k: (q * 3 + k) * PAD, 3, 0, lanes, zeros9())
+            accs = accumulate(y, lambda q, k: (q * 3 + k) * PAD, star_coefs, lanes, zeros9())
             for p in range(NQ):
                 rows = slice(PAD * p, PAD * (p + 1))
                 buf[rows, lanes] = src[rows, lanes] + w1(lanes) * x1[rows, lanes] + w2(lanes) * accs[p]
@@ -133,18 +169,22 @@
             pieces += list(halves(field[GROUP * g : GROUP * (g + 1), :]))
         return jnp.concatenate(pieces, axis=0).astype(BF16)
 
-    def copies(turn):
-        return [
-            pltpu.make_async_remote_copy(
-                src_ref=send.at[turn, j],
-                dst_ref=recv.at[turn, j],
-                send_sem=ssem.at[turn, j],
-                recv_sem=rsem.at[turn, j],
-                device_id=(lax.rem(me + o + n, n),),
-                device_id_type=MESH,
-            )
-            for j, o in enumerate(OFFSETS)
-        ]
+    def exchange(turn, j):
+        return pltpu.make_async_remote_copy(
+            src_ref=send.at[turn, j],
+            dst_ref=recv.at[turn, j],
+            send_sem=ssem.at[turn, j],
+            recv_sem=rsem.at[turn, j],
+            device_id=(me + OFFSETS[j],),
+            device_id_type=MESH,
+        )
+
+    def each(act, turn, sign):
+        for j, o in enumerate(OFFSETS):
+
+            @pl.when(inside(me + sign * o))
+            def _():
+                act(exchange(turn, j))
 
     low = iota((TOP, 128), 1) < NB
 
@@ -160,12 +200,10 @@
             lower = packed[ROWS - TOP : ROWS, 128 * t : 128 * t + 128]
             send[turn, 2 * t] = jnp.where(low, upper, pltpu.roll(lower, NB, 1))
             send[turn, 2 * t + 1] = jnp.where(low, pltpu.roll(upper, NB, 1), lower)
-        for copy in copies(turn):
-            copy.start()
+        each(lambda copy: copy.start(), turn, 1)
 
     def end_exchange(turn):
-        for copy in copies(turn):
-            copy.wait_recv()
+        each(lambda copy: copy.wait_recv(), turn, -1)
         for t in range(2):
             one, two = recv[turn, 2 * t], recv[turn, 2 * t + 1]
             lanes = slice(128 * t, 128 * t + 128)
@@ -191,36 +229,33 @@
                     z[row : row + PAD, :] = chosen
 
     def own_sum(lanes):
-        return accumulate(y, lambda q, k: (q * 7 + k) * PAD, 7, 0, lanes, zeros9())
+        return accumulate(y, lambda q, k: (q * 7 + k) * PAD, own_coefs, lanes, zeros9())
 
     def far_sum(lanes, accs):
-        return accumulate(z, lambda q, k: k * ROWS + q * PAD, 4, 7, lanes, accs)
+        return accumulate(z, lambda q, k: k * ROWS + q * PAD, far_coefs, lanes, accs)
 
     predictor(x, lambda lanes: 0.5, lambda lanes: 1.0 / 6.0)
-    pl.semaphore_wait(barrier, len(OFFSETS))
+    pl.semaphore_wait(barrier, partners)
     start_exchange(0)
+    arrived(f_plus, f_minus, flux_l, flux_n, neigh, nface, clus, to_p, from_p)
 
     def widen_flux(q, _):
-        for f in range(4):
-            coef[3 + f, q] = flux_l[f, q].astype(F32)
-            coef[7 + f, q] = flux_n[f, q].astype(F32)
+        coef_l[q] = flux_l[q].astype(F32)
+        coef_n[q] = flux_n[q].astype(F32)
         return 0
 
     lax.fori_loop(0, NQ, widen_flux, 0)
-    bd_o[...] = left_side([transposed(kst[d]) for d in range(3)] + [-f_minus[f] for f in range(4)])
+    bd_o[...] = left_side([transposed(kst[d]) for d in range(3)] + [-f_minus[:, f, :] for f in range(4)])
     for f in range(4):
-        bd_f[f] = left_side([-f_plus[f, h] for h in range(4)])
+        bd_f[f] = left_side([-f_plus[f, :, h, :] for h in range(4)])
     bd_p[0] = left_side([to_p[...]])
     bd_p[1] = left_side([from_p[...]])
     for f in range(4):
         wanted = neigh[f : f + 1, :]
         onehot[f, 0:E, :] = (iota((E, E), 0) == wanted).astype(F32).astype(BF16)
-        for j, o in enumerate(OFFSETS):
-            source = me - o
-            inside = (source >= 0) & (source < n)
-            base = jnp.where(inside, E + NB * j, -4 * E)
+        for j in range(4):
             rows = slice(E + NB * j, E + NB * (j + 1))
-            onehot[f, rows, :] = ((iota((NB, E), 0) + base) == wanted).astype(F32).astype(BF16)
+            onehot[f, rows, :] = ((iota((NB, E), 0) + E + NB * j) == wanted).astype(F32).astype(BF16)
 
     own_side()
     for t in range(2):
@@ -253,7 +288,8 @@
         for p in range(NQ):
             rows = slice(PAD * p, PAD * (p + 1))
             c1[rows, lanes] = c1[rows, lanes] + accs[p]
-    listed = (iota((E, E), 0) == dmg[...]) & (iota((E, E), 1) < count[0])
+    arrived(dmg, ymask, coh)
+    listed = (iota((E, E), 0) == dmg[...]) & (iota((E, E), 1) < h_count[...])
     live = lax.dot_general(
         jnp.ones((8, E), BF16), listed.astype(F32).astype(BF16), (((1,), (1,)), ((), ())), preferred_element_type=F32
     )[0:1]
@@ -289,24 +325,43 @@
     for q in range(6, NQ):
         out[q] = c1[PAD * q : PAD * q + NBAS, :]
     for turn in range(2):
-        for copy in copies(turn):
-            copy.wait_send()
+        each(lambda copy: copy.wait_send(), turn, 1)
 
 
 def per_device(n, dof, star, flux_l, flux_n, kst, fm, fp, neigh, nface, clus, send_l, dmg, count, ymask, coh, to_p, from_p):
+    operands = (dof, *(jnp.transpose(a, (1, 2, 0, 3)) for a in (star, flux_l, flux_n)), kst, jnp.transpose(fm, (1, 0, 2)), jnp.transpose(fp, (0, 2, 1, 3)), neigh, nface, clus.reshape(1, E), send_l, dmg, count.reshape(1, 1), ymask, coh.reshape(1, E), to_p, from_p)
+    hbm = pl.BlockSpec(memory_space=pltpu.HBM)
     vmem = pl.BlockSpec(memory_space=pltpu.VMEM)
-    smem = pl.BlockSpec(memory_space=pltpu.SMEM)
     return pl.pallas_call(
         functools.partial(kernel, n),
         out_shape=jax.ShapeDtypeStruct((NQ, NBAS, E), F32),
-        in_specs=[vmem] * 12 + [smem] + [vmem] * 4,
+        in_specs=[hbm] * 12 + [vmem] + [hbm] * 4,
         out_specs=vmem,
         scratch_shapes=[
+            pltpu.VMEM((NQ, NBAS, E), F32),
+            pltpu.VMEM((NQ, NQ, 3, E), BF16),
+            pltpu.VMEM((NQ, NQ, 4, E), BF16),
+            pltpu.VMEM((NQ, NQ, 4, E), BF16),
+            pltpu.VMEM((3, NBAS, NBAS), F32),
+            pltpu.VMEM((NBAS, 4, NBAS), F32),
+            pltpu.VMEM((4, NBAS, 4, NBAS), F32),
+            pltpu.VMEM((4, E), jnp.int32),
+            pltpu.VMEM((4, E), jnp.int32),
+            pltpu.VMEM((1, E), jnp.int32),
+            pltpu.VMEM((1, 4, NB), jnp.int32),
+            pltpu.VMEM((1, E), jnp.int32),
+            pltpu.VMEM((NBAS, E), jnp.int32),
+            pltpu.VMEM((1, E), F32),
+            pltpu.VMEM((NBAS, NBAS), F32),
+            pltpu.VMEM((NBAS, NBAS), F32),
+            pltpu.SemaphoreType.DMA((17,)),
             pltpu.VMEM((3 * GROUP, 256), BF16),
             pltpu.VMEM((7 * GROUP, 256), BF16),
             pltpu.VMEM((4, 4 * GROUP, 256), BF16),
             pltpu.VMEM((2, GROUP, 256), BF16),
-            pltpu.VMEM((11, NQ, NQ, E), F32),
+            pltpu.VMEM((NQ, NQ, 3, E), F32),
+            pltpu.VMEM((NQ, NQ, 4, E), F32),
+            pltpu.VMEM((NQ, NQ, 4, E), F32),
             pltpu.VMEM((4, 2 * E, E), BF16),
             pltpu.VMEM((E, E), BF16),
             pltpu.VMEM((ROWS, E), F32),
@@ -324,10 +379,10 @@
             pltpu.SemaphoreType.DMA((2, 4)),
         ],
         compiler_params=pltpu.CompilerParams(
-            collective_id=0, has_side_effects=True, vmem_limit_bytes=40 << 20
+            collective_id=0, has_side_effects=True, vmem_limit_bytes=48 << 20
         ),
         name="ader_cycle",
-    )(dof, star, flux_l, flux_n, kst, fm, fp, neigh, nface, clus.reshape(1, E), send_l, dmg, count, ymask, coh.reshape(1, E), to_p, from_p)
+    )(*(a if a.size == 1 else pltpu.with_memory_space_constraint(a, pltpu.HBM) for a in operands))
 
 
 def solution(mesh):

time: 40.6 us -> 32.6 us (0.80)
  the two profiles are of different devices: /device:TPU:1 before, /device:TPU:24 now
where the time goes in v2:
time: 32.6 us; the launch traced here: 32.5 us
  Pallas kernels  31.1 us (95%)
  local copies, waits for them, and re-layouts  0.69 us (2%)
  between operations  0.66 us (2%)
    pallas_call x1, Pallas kernels, per_device(): pl.pallas_call(functools.partial(kernel, n), out_shape=jax.ShapeDtypeStru...  31.1 us
    unnamed x1, local copies, waits for them, and re-layouts  0.69 us

profile of v2, /device:TPU:24, one launch (start us, length us, event | category | flops | bytes accessed | tf_op | source)
XLA Modules:
  0.0 32.5 jit_solution(13515655071396100665)
XLA Ops:
  0.7 31.1 %ader_cycle.1 = f32[9,20,256]{2,1,0:T(8,128)S(1)} custom-call(f32[9,20,256]{2,1,0:T(8,128)} %h_dof.1, bf16[9,9,3,256]{3,2,1,0:T(4,128)(2,1)} %bitcast.9, bf16[9,9,4,256]{3,2,1,0:T(4,128)(2,1)} %bitcast.10, bf16[9,9,4,256]{3,2,1,0:T(4,128)(2,1)} %bitcast.11, f32[3,20,20]{2,1,0:T(8,128)} %h_kst.1, f32[20,4,20]{2,1,0:T(4,128)} %bitcast.13, ...), custom_call_target="tpu_custom_call" | custom-call | tf_op jit(solution)/shard_map/ader_cycle/pallas_call | solution.py:335
  31.8 0.7 %copy.20 = f32[9,20,256]{2,1,0:T(8,128)} copy(f32[9,20,256]{2,1,0:T(8,128)S(1)} %ader_cycle.1) | data formatting | bytes 368640

commit v3 on v2

--- a/solution.py
+++ b/solution.py
@@ -67,7 +67,7 @@
     n, h_dof, h_star, h_flux_l, h_flux_n, h_kst, h_minus, h_plus, h_neigh, h_nface, h_clus, h_send, h_dmg, h_count, h_ymask, h_coh,
     h_to, h_from, out,
     dof, star, flux_l, flux_n, kst, f_minus, f_plus, neigh, nface, clus, send_l, dmg, ymask, coh, to_p, from_p, isem,
-    bd_d, bd_o, bd_f, bd_p, coef_s, coef_l, coef_n, onehot, onehot_s, x, x1, st, buf, c1, y, z, ext, ghost, send, recv, ssem, rsem,
+    bd_d, bd_o, bd_f, bd_p, coef_s, coef_l, coef_n, onehot, onehot_s, x, x1, st, buf, c1, part, y, z, ext, near, ghost, send, recv, ssem, rsem,
 ):
     me = lax.axis_index("dom")
     pairs = (
@@ -123,45 +123,56 @@
             lanes = slice(128 * (j // 2), 128 * (j // 2) + 128)
             onehot_s[:, lanes] = (iota((E, 128), 0) == both).astype(F32).astype(BF16)
 
-    def spread(src, lhs, dst):
+    def tiles():
+        return [slice(0, 128), slice(128, 256)]
+
+    def spread(src, lhs, dst, g):
         rows = lhs.shape[0]
+        dst[rows * g : rows * (g + 1), :] = dot(lhs[...], right_side(*halves(src[GROUP * g : GROUP * (g + 1), :])))
+
+    def accumulate(y_ref, row_of, coefs, quantities, lanes, accs):
+        accs = list(accs)
+        for q in quantities:
+            for k, (coef, i) in enumerate(coefs):
+                yv = y_ref[row_of(q, k) : row_of(q, k) + PAD, lanes]
+                for p in range(NQ):
+                    term = yv * coef[q, p, i : i + 1, lanes]
+                    accs[p] = term if accs[p] is None else accs[p] + term
+        return accs
+
+    def held(ref, lanes):
+        return [ref[PAD * p : PAD * (p + 1), lanes] for p in range(NQ)]
+
+    def hold(ref, lanes, accs):
+        for p in range(NQ):
+            ref[PAD * p : PAD * (p + 1), lanes] = accs[p]
+
+    def grouped(src, lhs, coefs, finish):
+        nk = len(coefs)
+        spread(src, lhs, y, 0)
         for g in range(3):
-            dst[rows * g : rows * (g + 1), :] = dot(
-                lhs[...], right_side(*halves(src[GROUP * g : GROUP * (g + 1), :]))
-            )
-
-    def accumulate(y_ref, row_of, coefs, lanes, accs):
-        def step(q, accs):
-            accs = list(accs)
-            for k, (coef, i) in enumerate(coefs):
-                yv = y_ref[pl.ds(pl.multiple_of(row_of(q, k), 8), PAD), lanes]
-                for p in range(NQ):
-                    accs[p] = accs[p] + yv * coef[q, p, i : i + 1, lanes]
-            return tuple(accs)
-
-        return lax.fori_loop(0, NQ, step, tuple(accs))
+            if g < 2:
+                spread(src, lhs, y, g + 1)
+            for lanes in tiles():
+                accs = [None] * NQ if g == 0 else held(part, lanes)
+                accs = accumulate(y, lambda q, k: (q * nk + k) * PAD, coefs, range(3 * g, 3 * g + 3), lanes, accs)
+                if g < 2:
+                    hold(part, lanes, accs)
+                else:
+                    finish(lanes, accs)
 
     star_coefs = [(coef_s, d) for d in range(3)]
     own_coefs = star_coefs + [(coef_l, f) for f in range(4)]
-    far_coefs = [(coef_n, f) for f in range(4)]
-
-    def zeros9():
-        return [jnp.zeros((PAD, 128), F32)] * NQ
 
     def predictor(src, w1, w2):
-        spread(src, bd_d, y)
-        for t in range(2):
-            lanes = slice(128 * t, 128 * t + 128)
-            accs = accumulate(y, lambda q, k: (q * 3 + k) * PAD, star_coefs, lanes, zeros9())
-            for p in range(NQ):
-                x1[PAD * p : PAD * (p + 1), lanes] = accs[p]
-        spread(x1, bd_d, y)
-        for t in range(2):
-            lanes = slice(128 * t, 128 * t + 128)
-            accs = accumulate(y, lambda q, k: (q * 3 + k) * PAD, star_coefs, lanes, zeros9())
+        grouped(src, bd_d, star_coefs, functools.partial(hold, x1))
+
+        def finish(lanes, accs):
             for p in range(NQ):
                 rows = slice(PAD * p, PAD * (p + 1))
                 buf[rows, lanes] = src[rows, lanes] + w1(lanes) * x1[rows, lanes] + w2(lanes) * accs[p]
+
+        grouped(x1, bd_d, star_coefs, finish)
 
     def split_field(field):
         pieces = []
@@ -211,28 +222,38 @@
             ghost[ROWS - TOP : ROWS, lanes] = jnp.where(low, pltpu.roll(one, NB, 1), two)
         ext[:, E : 2 * E] = split_field(ghost)
 
-    def own_side():
-        spread(buf, bd_o, y)
-
-    def far_side():
+    def own_side(finish):
+        grouped(buf, bd_o, own_coefs, finish)
+
+    def near_picks():
         for f in range(4):
-            here = [nface[f : f + 1, :] == h for h in range(3)]
-            picked = dot(ext[...], onehot[f])
-            for g in range(3):
-                hi = picked[2 * GROUP * g : 2 * GROUP * g + GROUP]
-                lo = picked[2 * GROUP * g + GROUP : 2 * GROUP * (g + 1)]
-                four = dot(bd_f[f], right_side(hi, lo))
-                for i in range(3):
-                    part = [four[PAD * (4 * i + h) : PAD * (4 * i + h + 1)] for h in range(4)]
-                    chosen = jnp.where(here[0], part[0], jnp.where(here[1], part[1], jnp.where(here[2], part[2], part[3])))
-                    row = f * ROWS + (3 * g + i) * PAD
-                    z[row : row + PAD, :] = chosen
-
-    def own_sum(lanes):
-        return accumulate(y, lambda q, k: (q * 7 + k) * PAD, own_coefs, lanes, zeros9())
-
-    def far_sum(lanes, accs):
-        return accumulate(z, lambda q, k: k * ROWS + q * PAD, far_coefs, lanes, accs)
+            near[f] = dot(ext[:, 0:E], onehot[f, 0:E, :]).astype(BF16)
+
+    def face(f):
+        here = [nface[f : f + 1, :] == h for h in range(3)]
+        picked = dot(ext[...], onehot[f])
+        for g in range(3):
+            hi = picked[2 * GROUP * g : 2 * GROUP * g + GROUP]
+            lo = picked[2 * GROUP * g + GROUP : 2 * GROUP * (g + 1)]
+            four = dot(bd_f[f], right_side(hi, lo))
+            for i in range(3):
+                part_h = [four[PAD * (4 * i + h) : PAD * (4 * i + h + 1)] for h in range(4)]
+                row = f * ROWS + (3 * g + i) * PAD
+                z[row : row + PAD, :] = jnp.where(
+                    here[0], part_h[0], jnp.where(here[1], part_h[1], jnp.where(here[2], part_h[2], part_h[3]))
+                )
+
+    def far_side(finish):
+        face(0)
+        for f in range(4):
+            if f < 3:
+                face(f + 1)
+            for lanes in tiles():
+                accs = accumulate(z, lambda q, k: f * ROWS + q * PAD, [(coef_n, f)], range(NQ), lanes, held(c1, lanes))
+                if f < 3:
+                    hold(c1, lanes, accs)
+                else:
+                    finish(lanes, accs)
 
     predictor(x, lambda lanes: 0.5, lambda lanes: 1.0 / 6.0)
     pl.semaphore_wait(barrier, partners)
@@ -257,17 +278,10 @@
             rows = slice(E + NB * j, E + NB * (j + 1))
             onehot[f, rows, :] = ((iota((NB, E), 0) + E + NB * j) == wanted).astype(F32).astype(BF16)
 
-    own_side()
-    for t in range(2):
-        lanes = slice(128 * t, 128 * t + 128)
-        accs = own_sum(lanes)
-        for p in range(NQ):
-            c1[PAD * p : PAD * (p + 1), lanes] = accs[p]
+    own_side(functools.partial(hold, c1))
     end_exchange(0)
-    far_side()
-    for t in range(2):
-        lanes = slice(128 * t, 128 * t + 128)
-        accs = far_sum(lanes, [c1[PAD * p : PAD * (p + 1), lanes] for p in range(NQ)])
+
+    def finish_one(lanes, accs):
         fine = clus[0:1, lanes] == 0
         for p in range(NQ):
             rows = slice(PAD * p, PAD * (p + 1))
@@ -276,30 +290,27 @@
             c1[rows, lanes] = total
             st[rows, lanes] = jnp.where(fine, total, start)
 
+    far_side(finish_one)
+
     def weight(fine_one, coarse_one):
         return lambda lanes: jnp.where(clus[0:1, lanes] == 0, F32(fine_one), F32(coarse_one))
 
     predictor(st, weight(0.5, 1.5), weight(1.0 / 6.0, 7.0 / 6.0))
     start_exchange(1)
-    own_side()
-    for t in range(2):
-        lanes = slice(128 * t, 128 * t + 128)
-        accs = own_sum(lanes)
+
+    def finish_two(lanes, accs):
         for p in range(NQ):
             rows = slice(PAD * p, PAD * (p + 1))
             c1[rows, lanes] = c1[rows, lanes] + accs[p]
+
+    own_side(finish_two)
     arrived(dmg, ymask, coh)
     listed = (iota((E, E), 0) == dmg[...]) & (iota((E, E), 1) < h_count[...])
     live = lax.dot_general(
         jnp.ones((8, E), BF16), listed.astype(F32).astype(BF16), (((1,), (1,)), ((), ())), preferred_element_type=F32
     )[0:1]
     end_exchange(1)
-    far_side()
-    for t in range(2):
-        lanes = slice(128 * t, 128 * t + 128)
-        accs = far_sum(lanes, [c1[PAD * p : PAD * (p + 1), lanes] for p in range(NQ)])
-        for p in range(NQ):
-            c1[PAD * p : PAD * (p + 1), lanes] = accs[p]
+    far_side(functools.partial(hold, c1))
 
     points = []
     for g in range(2):
@@ -369,9 +380,11 @@
             pltpu.VMEM((ROWS, E), F32),
             pltpu.VMEM((ROWS, E), F32),
             pltpu.VMEM((ROWS, E), F32),
+            pltpu.VMEM((ROWS, E), F32),
             pltpu.VMEM((7 * ROWS, E), F32),
             pltpu.VMEM((4 * ROWS, E), F32),
             pltpu.VMEM((2 * ROWS, 2 * E), BF16),
+            pltpu.VMEM((4, 2 * ROWS, E), BF16),
             pltpu.VMEM((ROWS, E), F32),
             pltpu.VMEM((2, 4, TOP, 128), F32),
             pltpu.VMEM((2, 4, TOP, 128), F32),

time: 32.6 us -> 31 us (0.951)
  Pallas kernels: 31.1 us -> 29.5 us
    pallas_call x1, Pallas kernels: 31.1 us -> 29.5 us  [per_device(): pl.pallas_call(functools.partial(kernel, n), out_shape=jax.ShapeDtypeStru...]
where the time goes in v3:
time: 31 us; the launch traced here: 30.8 us
  Pallas kernels  29.5 us (95%)
  local copies, waits for them, and re-layouts  0.69 us (2%)
  between operations  0.66 us (2%)
    pallas_call x1, Pallas kernels, per_device(): pl.pallas_call(functools.partial(kernel, n), out_shape=jax.ShapeDtypeStru...  29.5 us
    unnamed x1, local copies, waits for them, and re-layouts  0.69 us

profile of v3, /device:TPU:24, one launch (start us, length us, event | category | flops | bytes accessed | tf_op | source)
XLA Modules:
  0.0 30.8 jit_solution(6639628960251386691)
XLA Ops:
  0.7 29.5 %ader_cycle.1 = f32[9,20,256]{2,1,0:T(8,128)S(1)} custom-call(f32[9,20,256]{2,1,0:T(8,128)} %h_dof.1, bf16[9,9,3,256]{3,2,1,0:T(4,128)(2,1)} %bitcast.9, bf16[9,9,4,256]{3,2,1,0:T(4,128)(2,1)} %bitcast.10, bf16[9,9,4,256]{3,2,1,0:T(4,128)(2,1)} %bitcast.11, f32[3,20,20]{2,1,0:T(8,128)} %h_kst.1, f32[20,4,20]{2,1,0:T(4,128)} %bitcast.13, ...), custom_call_target="tpu_custom_call" | custom-call | tf_op jit(solution)/shard_map/ader_cycle/pallas_call | solution.py:346
  30.1 0.7 %copy.20 = f32[9,20,256]{2,1,0:T(8,128)} copy(f32[9,20,256]{2,1,0:T(8,128)S(1)} %ader_cycle.1) | data formatting | bytes 368640

commit v4 on v3

--- a/solution.py
+++ b/solution.py
@@ -14,7 +14,7 @@
 ROWS = NQ * PAD
 GROUP = 3 * PAD
 E, NB = 256, 64
-TOP = 112
+PAIRS, REST = 4, 12
 FRICTION, RELAXATION = 0.6, 0.5
 
 
@@ -67,9 +67,10 @@
     n, h_dof, h_star, h_flux_l, h_flux_n, h_kst, h_minus, h_plus, h_neigh, h_nface, h_clus, h_send, h_dmg, h_count, h_ymask, h_coh,
     h_to, h_from, out,
     dof, star, flux_l, flux_n, kst, f_minus, f_plus, neigh, nface, clus, send_l, dmg, ymask, coh, to_p, from_p, isem,
-    bd_d, bd_o, bd_f, bd_p, coef_s, coef_l, coef_n, onehot, onehot_s, x, x1, st, buf, c1, part, y, z, ext, near, ghost, send, recv, ssem, rsem,
+    bd_d, bd_o, bd_f, bd_p, coef_s, coef_l, coef_n, onehot, onehot_s, x, x1, st, buf, c1, part, y0, y1, y2, z0, z1, z2, z3, ext, near, ghost, send_a, send_b, recv_a, recv_b, ssem, rsem,
 ):
     me = lax.axis_index("dom")
+    y, z = (y0, y1, y2), (z0, z1, z2, z3)
     pairs = (
         (h_dof, dof), (h_kst, kst), (h_star, star), (h_send, send_l), (h_plus, f_plus), (h_minus, f_minus), (h_flux_l, flux_l),
         (h_flux_n, flux_n), (h_neigh, neigh), (h_nface, nface), (h_clus, clus), (h_to, to_p), (h_from, from_p),
@@ -98,10 +99,15 @@
     partners = sum(jnp.where(inside(me + o), 1, 0) for o in OFFSETS)
     for j, o in enumerate(OFFSETS):
 
+        for turn in range(2):
+            recv_a[turn, j, :, NBAS:PAD, :] = jnp.zeros((PAIRS, PAD - NBAS, 128), F32)
+            recv_b[turn, j, REST:16, :] = jnp.zeros((16 - REST, 128), F32)
+
         @pl.when(jnp.logical_not(inside(me - o)))
         def _():
             for turn in range(2):
-                recv[turn, j] = jnp.zeros((TOP, 128), F32)
+                recv_a[turn, j, :, 0:NBAS, :] = jnp.zeros((PAIRS, NBAS, 128), F32)
+                recv_b[turn, j, 0:REST, :] = jnp.zeros((REST, 128), F32)
 
     arrived(dof, kst, star)
     for q in range(NQ):
@@ -128,7 +134,7 @@
 
     def spread(src, lhs, dst, g):
         rows = lhs.shape[0]
-        dst[rows * g : rows * (g + 1), :] = dot(lhs[...], right_side(*halves(src[GROUP * g : GROUP * (g + 1), :])))
+        dst[g][0:rows, :] = dot(lhs[...], right_side(*halves(src[GROUP * g : GROUP * (g + 1), :])))
 
     def accumulate(y_ref, row_of, coefs, quantities, lanes, accs):
         accs = list(accs)
@@ -155,7 +161,7 @@
                 spread(src, lhs, y, g + 1)
             for lanes in tiles():
                 accs = [None] * NQ if g == 0 else held(part, lanes)
-                accs = accumulate(y, lambda q, k: (q * nk + k) * PAD, coefs, range(3 * g, 3 * g + 3), lanes, accs)
+                accs = accumulate(y[g], lambda q, k: ((q - 3 * g) * nk + k) * PAD, coefs, range(3 * g, 3 * g + 3), lanes, accs)
                 if g < 2:
                     hold(part, lanes, accs)
                 else:
@@ -181,23 +187,35 @@
         return jnp.concatenate(pieces, axis=0).astype(BF16)
 
     def exchange(turn, j):
-        return pltpu.make_async_remote_copy(
-            src_ref=send.at[turn, j],
-            dst_ref=recv.at[turn, j],
-            send_sem=ssem.at[turn, j],
-            recv_sem=rsem.at[turn, j],
-            device_id=(me + OFFSETS[j],),
-            device_id_type=MESH,
+        parts = (
+            (send_a.at[turn, j, :, 0:NBAS, :], recv_a.at[turn, j, :, 0:NBAS, :]),
+            (send_b.at[turn, j, 0:REST, :], recv_b.at[turn, j, 0:REST, :]),
         )
+        return [
+            pltpu.make_async_remote_copy(
+                src_ref=source,
+                dst_ref=target,
+                send_sem=ssem.at[turn, j, i],
+                recv_sem=rsem.at[turn, j, i],
+                device_id=(me + OFFSETS[j],),
+                device_id_type=MESH,
+            )
+            for i, (source, target) in enumerate(parts)
+        ]
 
     def each(act, turn, sign):
         for j, o in enumerate(OFFSETS):
 
             @pl.when(inside(me + sign * o))
             def _():
-                act(exchange(turn, j))
-
-    low = iota((TOP, 128), 1) < NB
+                for copy in exchange(turn, j):
+                    act(copy)
+
+    low = iota((PAD, 128), 1) < NB
+
+    def swap(one, two):
+        mask = low[0 : one.shape[0]]
+        return jnp.where(mask, one, pltpu.roll(two, NB, 1)), jnp.where(mask, pltpu.roll(one, NB, 1), two)
 
     def start_exchange(turn):
         ext[:, 0:E] = split_field(buf)
@@ -206,20 +224,28 @@
             [picked[2 * GROUP * g : 2 * GROUP * g + GROUP] + picked[2 * GROUP * g + GROUP : 2 * GROUP * (g + 1)] for g in range(3)],
             axis=0,
         )
-        for t in range(2):
-            upper = packed[0:TOP, 128 * t : 128 * t + 128]
-            lower = packed[ROWS - TOP : ROWS, 128 * t : 128 * t + 128]
-            send[turn, 2 * t] = jnp.where(low, upper, pltpu.roll(lower, NB, 1))
-            send[turn, 2 * t + 1] = jnp.where(low, pltpu.roll(upper, NB, 1), lower)
+        for t, lanes in enumerate(tiles()):
+            for i in range(PAIRS):
+                upper = packed[PAD * i : PAD * (i + 1), lanes]
+                lower = packed[PAD * (i + PAIRS) : PAD * (i + PAIRS + 1), lanes]
+                send_a[turn, 2 * t, i], send_a[turn, 2 * t + 1, i] = swap(upper, lower)
+            last = packed[8 * PAD : ROWS, lanes]
+            send_b[turn, 2 * t, 0:8, :], send_b[turn, 2 * t + 1, 0:8, :] = swap(last[0:8], last[8:16])
+            send_b[turn, 2 * t, 8:16, :], send_b[turn, 2 * t + 1, 8:16, :] = last[16:24], pltpu.roll(last[16:24], NB, 1)
         each(lambda copy: copy.start(), turn, 1)
 
     def end_exchange(turn):
         each(lambda copy: copy.wait_recv(), turn, -1)
-        for t in range(2):
-            one, two = recv[turn, 2 * t], recv[turn, 2 * t + 1]
-            lanes = slice(128 * t, 128 * t + 128)
-            ghost[0:TOP, lanes] = jnp.where(low, one, pltpu.roll(two, NB, 1))
-            ghost[ROWS - TOP : ROWS, lanes] = jnp.where(low, pltpu.roll(one, NB, 1), two)
+        for t, lanes in enumerate(tiles()):
+            for i in range(PAIRS):
+                upper, lower = swap(recv_a[turn, 2 * t, i], recv_a[turn, 2 * t + 1, i])
+                ghost[PAD * i : PAD * (i + 1), lanes] = upper
+                ghost[PAD * (i + PAIRS) : PAD * (i + PAIRS + 1), lanes] = lower
+            one, two = recv_b[turn, 2 * t], recv_b[turn, 2 * t + 1]
+            upper, lower = swap(one[0:8], two[0:8])
+            ghost[8 * PAD : 8 * PAD + 8, lanes] = upper
+            ghost[8 * PAD + 8 : 8 * PAD + 16, lanes] = lower
+            ghost[8 * PAD + 16 : ROWS, lanes] = swap(one[8:16], two[8:16])[0]
         ext[:, E : 2 * E] = split_field(ghost)
 
     def own_side(finish):
@@ -238,22 +264,19 @@
             four = dot(bd_f[f], right_side(hi, lo))
             for i in range(3):
                 part_h = [four[PAD * (4 * i + h) : PAD * (4 * i + h + 1)] for h in range(4)]
-                row = f * ROWS + (3 * g + i) * PAD
-                z[row : row + PAD, :] = jnp.where(
+                row = (3 * g + i) * PAD
+                z[f][row : row + PAD, :] = jnp.where(
                     here[0], part_h[0], jnp.where(here[1], part_h[1], jnp.where(here[2], part_h[2], part_h[3]))
                 )
 
     def far_side(finish):
-        face(0)
         for f in range(4):
-            if f < 3:
-                face(f + 1)
-            for lanes in tiles():
-                accs = accumulate(z, lambda q, k: f * ROWS + q * PAD, [(coef_n, f)], range(NQ), lanes, held(c1, lanes))
-                if f < 3:
-                    hold(c1, lanes, accs)
-                else:
-                    finish(lanes, accs)
+            face(f)
+        for lanes in tiles():
+            accs = held(c1, lanes)
+            for f in range(4):
+                accs = accumulate(z[f], lambda q, k: q * PAD, [(coef_n, f)], range(NQ), lanes, accs)
+            finish(lanes, accs)
 
     predictor(x, lambda lanes: 0.5, lambda lanes: 1.0 / 6.0)
     pl.semaphore_wait(barrier, partners)
@@ -381,15 +404,17 @@
             pltpu.VMEM((ROWS, E), F32),
             pltpu.VMEM((ROWS, E), F32),
             pltpu.VMEM((ROWS, E), F32),
-            pltpu.VMEM((7 * ROWS, E), F32),
-            pltpu.VMEM((4 * ROWS, E), F32),
+            *([pltpu.VMEM((7 * GROUP, E), F32)] * 3),
+            *([pltpu.VMEM((ROWS, E), F32)] * 4),
             pltpu.VMEM((2 * ROWS, 2 * E), BF16),
             pltpu.VMEM((4, 2 * ROWS, E), BF16),
             pltpu.VMEM((ROWS, E), F32),
-            pltpu.VMEM((2, 4, TOP, 128), F32),
-            pltpu.VMEM((2, 4, TOP, 128), F32),
-            pltpu.SemaphoreType.DMA((2, 4)),
-            pltpu.SemaphoreType.DMA((2, 4)),
+            pltpu.VMEM((2, 4, PAIRS, PAD, 128), F32),
+            pltpu.VMEM((2, 4, 16, 128), F32),
+            pltpu.VMEM((2, 4, PAIRS, PAD, 128), F32),
+            pltpu.VMEM((2, 4, 16, 128), F32),
+            pltpu.SemaphoreType.DMA((2, 4, 2)),
+            pltpu.SemaphoreType.DMA((2, 4, 2)),
         ],
         compiler_params=pltpu.CompilerParams(
             collective_id=0, has_side_effects=True, vmem_limit_bytes=48 << 20

time: 31 us -> 30.9 us (level)
  no operation moved by 1% of the time
where the time goes in v4:
time: 30.9 us; the launch traced here: 30.7 us
  Pallas kernels  29.4 us (95%)
  local copies, waits for them, and re-layouts  0.69 us (2%)
  between operations  0.66 us (2%)
    pallas_call x1, Pallas kernels, per_device(): pl.pallas_call(functools.partial(kernel, n), out_shape=jax.ShapeDtypeStru...  29.4 us
    unnamed x1, local copies, waits for them, and re-layouts  0.69 us

profile of v4, /device:TPU:24, one launch (start us, length us, event | category | flops | bytes accessed | tf_op | source)
XLA Modules:
  0.0 30.7 jit_solution(8713138206503376086)
XLA Ops:
  0.7 29.4 %ader_cycle.1 = f32[9,20,256]{2,1,0:T(8,128)S(1)} custom-call(f32[9,20,256]{2,1,0:T(8,128)} %h_dof.1, bf16[9,9,3,256]{3,2,1,0:T(4,128)(2,1)} %bitcast.9, bf16[9,9,4,256]{3,2,1,0:T(4,128)(2,1)} %bitcast.10, bf16[9,9,4,256]{3,2,1,0:T(4,128)(2,1)} %bitcast.11, f32[3,20,20]{2,1,0:T(8,128)} %h_kst.1, f32[20,4,20]{2,1,0:T(4,128)} %bitcast.13, ...), custom_call_target="tpu_custom_call" | custom-call | tf_op jit(solution)/shard_map/ader_cycle/pallas_call | solution.py:369
  30.0 0.7 %copy.20 = f32[9,20,256]{2,1,0:T(8,128)} copy(f32[9,20,256]{2,1,0:T(8,128)S(1)} %ader_cycle.1) | data formatting | bytes 368640

commit v5 on v3

--- a/solution.py
+++ b/solution.py
@@ -191,7 +191,8 @@
         )
 
     def each(act, turn, sign):
-        for j, o in enumerate(OFFSETS):
+        for j in (2, 0, 3, 1):
+            o = OFFSETS[j]
 
             @pl.when(inside(me + sign * o))
             def _():

time: 31 us -> 31.3 us (level)
    pallas_call x1, Pallas kernels: 29.5 us -> 29.8 us  [per_device(): pl.pallas_call(functools.partial(kernel, n), out_shape=jax.ShapeDtypeStru...]
where the time goes in v5:
time: 31.3 us; the launch traced here: 31.2 us
  Pallas kernels  29.8 us (95%)
  local copies, waits for them, and re-layouts  0.69 us (2%)
  between operations  0.66 us (2%)
    pallas_call x1, Pallas kernels, per_device(): pl.pallas_call(functools.partial(kernel, n), out_shape=jax.ShapeDtypeStru...  29.8 us
    unnamed x1, local copies, waits for them, and re-layouts  0.69 us

profile of v5, /device:TPU:24, one launch (start us, length us, event | category | flops | bytes accessed | tf_op | source)
XLA Modules:
  0.0 31.2 jit_solution(2813280984584894865)
XLA Ops:
  0.7 29.8 %ader_cycle.1 = f32[9,20,256]{2,1,0:T(8,128)S(1)} custom-call(f32[9,20,256]{2,1,0:T(8,128)} %h_dof.1, bf16[9,9,3,256]{3,2,1,0:T(4,128)(2,1)} %bitcast.9, bf16[9,9,4,256]{3,2,1,0:T(4,128)(2,1)} %bitcast.10, bf16[9,9,4,256]{3,2,1,0:T(4,128)(2,1)} %bitcast.11, f32[3,20,20]{2,1,0:T(8,128)} %h_kst.1, f32[20,4,20]{2,1,0:T(4,128)} %bitcast.13, ...), custom_call_target="tpu_custom_call" | custom-call | tf_op jit(solution)/shard_map/ader_cycle/pallas_call | solution.py:347
  30.5 0.7 %copy.20 = f32[9,20,256]{2,1,0:T(8,128)} copy(f32[9,20,256]{2,1,0:T(8,128)S(1)} %ader_cycle.1) | data formatting | bytes 368640
